TPU v7x, 256 devices: a whole 4x4x8 slice. The times are simulated.
256 devices in a mesh: dp: 16 (over z_hi, y, core), seq: 16 (over x, z_lo).
Axes of the slice: x: 4, y: 4, z: 8 (z_hi: 2, z_lo: 4; z = z_hi * 4 + z_lo), core: 2. Of those that a mesh axis runs over, the one named last changes fastest.
Arguments:
- inputs: bfloat16 [2, 65536, 2048], P(None, 'seq', 'dp'), may hold values from -6 to 6
- cotangent: bfloat16 [2, 65536, 2048], P(None, 'seq', 'dp'), may hold values from -6 to 6
- kernel: bfloat16 [65536, 2048], P('seq', 'dp'), may hold values from -6 to 6
- factor_one: bfloat16 [256, 256], replicated, may hold values from -0.375 to 0.375
- factor_two: bfloat16 [256, 256], replicated, may hold values from -0.375 to 0.375
Outputs:
- grad_inputs: bfloat16 [2, 65536, 2048], P(None, 'seq', 'dp')
- grad_kernel: bfloat16 [65536, 2048], P('seq', 'dp')
- grad_factor_one: float32 [256, 256], replicated
- grad_factor_two: float32 [256, 256], replicated
All inputs are finite; a program needn't handle non-finite values.
Results may differ from a plain program's by a relative error of at most 0.0085.
Values may be sent and summed in bfloat16 or wider, within the bound.
A program may use at most 128 MiB of HBM per device.

v0:
```python
import math
import jax
import jax.numpy as jnp
from jax import lax
from jax.sharding import PartitionSpec as P


def within_blocks(factor, values):
    return jnp.einsum("cb,nabh->nach", factor, values, preferred_element_type=jnp.float32)


def within_blocks_back(factor, values):
    return jnp.einsum("cb,nach->nabh", factor, values, preferred_element_type=jnp.float32)


def across_blocks(factor, values):
    return jnp.einsum("ea,nach->nech", factor, values, preferred_element_type=jnp.float32)


def across_blocks_back(factor, values):
    return jnp.einsum("ea,nech->nach", factor, values, preferred_element_type=jnp.float32)


def pair_product(left, right):
    return jnp.einsum("nech,nach->ea", left, right, preferred_element_type=jnp.float32)


def on_device(inputs, cotangent, kernel, factor_one, factor_two):
    batch_count = inputs.shape[0]
    row_count = inputs.shape[1]
    channels = inputs.shape[2]
    block_size = factor_one.shape[0]
    block_count = factor_two.shape[0]
    local_blocks = row_count // block_size
    inputs_cube = inputs.reshape(batch_count, local_blocks, block_size, channels)
    grads_cube = cotangent.reshape(batch_count, local_blocks, block_size, channels)
    kernel_cube = kernel.reshape(local_blocks, block_size, channels)
    within_mix = within_blocks(factor_one, inputs_cube).astype(jnp.bfloat16)
    within_spread = lax.all_to_all(within_mix, "seq", split_axis=2, concat_axis=1, tiled=True)
    spectrum = across_blocks(factor_two, within_spread).astype(jnp.bfloat16)
    grad_within = within_blocks(factor_one, grads_cube).astype(jnp.bfloat16)
    grad_spread = lax.all_to_all(grad_within, "seq", split_axis=2, concat_axis=1, tiled=True)
    grad_spectrum = across_blocks(factor_two, grad_spread).astype(jnp.bfloat16)
    spectrum_home, grad_spectrum_home = (
        lax.all_to_all(spectrum, "seq", split_axis=1, concat_axis=2, tiled=True),
        lax.all_to_all(grad_spectrum, "seq", split_axis=1, concat_axis=2, tiled=True),
    )
    kernel_wide = kernel_cube.astype(jnp.float32)[None]
    weighted_home = (kernel_wide * spectrum_home.astype(jnp.float32)).astype(jnp.bfloat16)
    grad_weighted_home = (kernel_wide * grad_spectrum_home.astype(jnp.float32)).astype(jnp.bfloat16)
    kernel_terms = jnp.sum(
        grad_spectrum_home.astype(jnp.float32) * spectrum_home.astype(jnp.float32), axis=0
    )
    weighted, grad_weighted = (
        lax.all_to_all(weighted_home, "seq", split_axis=2, concat_axis=1, tiled=True),
        lax.all_to_all(grad_weighted_home, "seq", split_axis=2, concat_axis=1, tiled=True),
    )
    returned_spread = across_blocks_back(factor_two, weighted).astype(jnp.bfloat16)
    grad_returned_spread = across_blocks_back(factor_two, grad_weighted).astype(jnp.bfloat16)
    second_terms = pair_product(weighted, grad_spread) + pair_product(grad_weighted, within_spread)
    returned, grad_returned = (
        lax.all_to_all(returned_spread, "seq", split_axis=1, concat_axis=2, tiled=True),
        lax.all_to_all(grad_returned_spread, "seq", split_axis=1, concat_axis=2, tiled=True),
    )
    grad_inputs = within_blocks_back(factor_one, grad_returned).astype(jnp.bfloat16)
    first_terms = jnp.einsum(
        "nach,nabh->cb", returned, grads_cube, preferred_element_type=jnp.float32
    )
    first_terms = first_terms + jnp.einsum(
        "nach,nabh->cb", grad_returned, inputs_cube, preferred_element_type=jnp.float32
    )
    first_total, second_total = lax.psum((first_terms, second_terms), ("dp", "seq"))
    kernel_half = kernel_terms.astype(jnp.bfloat16)
    grad_kernel = kernel_half.reshape(row_count, channels)
    full_width = channels * lax.axis_size("dp")
    scale_first = 1.0 / math.sqrt(batch_count * block_count * full_width)
    scale_second = 1.0 / math.sqrt(batch_count * block_size * full_width)
    return (
        grad_inputs.reshape(batch_count, row_count, channels),
        grad_kernel,
        first_total * scale_first,
        second_total * scale_second,
    )


def solution(mesh):
    return jax.shard_map(
        on_device,
        mesh=mesh,
        in_specs=(P(None, "seq", "dp"), P(None, "seq", "dp"), P("seq", "dp"), P(), P()),
        out_specs=(P(None, "seq", "dp"), P("seq", "dp"), P(), P()),
        check_vma=False,
    )
```

profile of v0, /device:TPU:2, one launch (start us, length us, event | category | flops | bytes accessed | tf_op | source)
XLA Modules:
  0.0 732.7 jit_solution(2225070951256302418)
XLA Ops:
  11.0 4.6 copy.99
  15.6 9.0 %all-to-all-start.4 = ((bf16[2,16,256,128]{3,1,0,2:T(8,128)(2,1)}), bf16[2,16,256,128]{3,1,0,2:T(8,128)(2,1)}, u32[]{:S(2)}, u32[]{:S(2)}) async-start(bf16[2,16,256,128]{3,1,0,2:T(8,128)(2,1)} %copy.99), calls=%async_computation.4 | async-start | bytes 4194304 | tf_op jit(solution)/shard_map/all_to_all | solution.py:39
  26.7 4.6 copy.82
  31.3 41.4 %all-to-all-done.4 = bf16[2,16,256,128]{3,1,0,2:T(8,128)(2,1)} async-done(((bf16[2,16,256,128]{3,1,0,2:T(8,128)(2,1)}), bf16[2,16,256,128]{3,1,0,2:T(8,128)(2,1)}, u32[]{:S(2)}, u32[]{:S(2)}) %all-to-all-start.4) | async-done | bytes 2097184 | tf_op jit(solution)/shard_map/all_to_all | solution.py:39
  72.6 6.7 all-to-all-start
  85.6 4.5 copy.103
  90.1 36.7 %all-to-all-done = bf16[2,16,256,128]{3,1,0,2:T(8,128)(2,1)} async-done(((bf16[2,16,256,128]{3,1,0,2:T(8,128)(2,1)}), bf16[2,16,256,128]{3,1,0,2:T(8,128)(2,1)}, u32[]{:S(2)}, u32[]{:S(2)}) %all-to-all-start) | async-done | bytes 2097184 | tf_op jit(solution)/shard_map/all_to_all | solution.py:42
  126.8 6.8 all-to-all-start.5
  139.9 4.5 copy.86
  144.4 36.7 %all-to-all-done.5 = bf16[2,256,16,128]{3,2,0,1:T(8,128)(2,1)} async-done(((bf16[2,256,16,128]{3,2,0,1:T(8,128)(2,1)}), bf16[2,256,16,128]{3,2,0,1:T(8,128)(2,1)}, u32[]{:S(2)}, u32[]{:S(2)}) %all-to-all-start.5) | async-done | bytes 2097184 | tf_op jit(solution)/shard_map/all_to_all | solution.py:45
  181.1 6.9 all-to-all-start.1
  195.1 40.3 %all-to-all-done.1 = bf16[2,256,16,128]{3,2,0,1:T(8,128)(2,1)} async-done(((bf16[2,256,16,128]{3,2,0,1:T(8,128)(2,1)}), bf16[2,256,16,128]{3,2,0,1:T(8,128)(2,1)}, u32[]{:S(2)}, u32[]{:S(2)}) %all-to-all-start.1) | async-done | bytes 2097184 | tf_op jit(solution)/shard_map/all_to_all | solution.py:46
  245.3 6.8 all-to-all-start.6
  252.1 4.3 copy.89
  256.4 43.2 %all-to-all-done.6 = bf16[2,16,256,128]{3,1,0,2:T(8,128)(2,1)} async-done(((bf16[2,16,256,128]{3,1,0,2:T(8,128)(2,1)}), bf16[2,16,256,128]{3,1,0,2:T(8,128)(2,1)}, u32[]{:S(2)}, u32[]{:S(2)}) %all-to-all-start.6) | async-done | bytes 2097184 | tf_op jit(solution)/shard_map/all_to_all | solution.py:55
  299.6 6.8 all-to-all-start.2
  312.6 4.6 copy.113
  317.1 36.8 %all-to-all-done.2 = bf16[2,16,256,128]{3,1,0,2:T(8,128)(2,1)} async-done(((bf16[2,16,256,128]{3,1,0,2:T(8,128)(2,1)}), bf16[2,16,256,128]{3,1,0,2:T(8,128)(2,1)}, u32[]{:S(2)}, u32[]{:S(2)}) %all-to-all-start.2) | async-done | bytes 2097184 | tf_op jit(solution)/shard_map/all_to_all | solution.py:56
  353.9 6.8 all-to-all-start.7
  367.0 4.5 copy.93
  371.5 36.8 %all-to-all-done.7 = bf16[2,256,16,128]{3,2,0,1:T(8,128)(2,1)} async-done(((bf16[2,256,16,128]{3,2,0,1:T(8,128)(2,1)}), bf16[2,256,16,128]{3,2,0,1:T(8,128)(2,1)}, u32[]{:S(2)}, u32[]{:S(2)}) %all-to-all-start.7) | async-done | bytes 2097184 | tf_op jit(solution)/shard_map/all_to_all | solution.py:62
  408.3 6.8 all-to-all-start.3
  431.5 31.1 %all-to-all-done.3 = bf16[2,256,16,128]{3,2,0,1:T(8,128)(2,1)} async-done(((bf16[2,256,16,128]{3,2,0,1:T(8,128)(2,1)}), bf16[2,256,16,128]{3,2,0,1:T(8,128)(2,1)}, u32[]{:S(2)}, u32[]{:S(2)}) %all-to-all-start.3) | async-done | bytes 2097184 | tf_op jit(solution)/shard_map/all_to_all | solution.py:63
  475.4 248.7 %all-reduce.3.cloned.1.call-done = (f32[256,256]{1,0:T(8,128)}, f32[256,256]{1,0:T(8,128)}) async-done(((f32[256,256]{1,0:T(8,128)}, f32[256,256]{1,0:T(8,128)}), (f32[256,256]{1,0:T(8,128)}, f32[256,256]{1,0:T(8,128)})) %all-reduce.3.cloned.1.call-update) | async-done | bytes 524304 | tf_op jit(solution)/shard_map/psum | solution.py:72
  (60 shorter events, 78.5 us)
Async XLA Ops:
  7.2 17.4 %copy-start = (bf16[2,4096,128]{2,1,0:T(8,128)(2,1)S(1)}, bf16[2,4096,128]{2,1,0:T(8,128)(2,1)}, u32[]{:S(2)}) copy-start(bf16[2,4096,128]{2,1,0:T(8,128)(2,1)} %param.6) | copy-start | bytes 6291460
  15.6 9.0 %copy-start.13 = (bf16[256,256]{1,0:T(8,128)(2,1)S(1)}, bf16[256,256]{1,0:T(8,128)(2,1)}, u32[]{:S(2)}) copy-start(bf16[256,256]{1,0:T(8,128)(2,1)} %param.8) | copy-start | bytes 393220
  15.6 57.0 %all-to-all-start.4 = ((bf16[2,16,256,128]{3,1,0,2:T(8,128)(2,1)}), bf16[2,16,256,128]{3,1,0,2:T(8,128)(2,1)}, u32[]{:S(2)}, u32[]{:S(2)}) async-start(bf16[2,16,256,128]{3,1,0,2:T(8,128)(2,1)} %copy.99), calls=%async_computation.4 | async-start | bytes 4194304 | tf_op jit(solution)/shard_map/all_to_all | solution.py:39
  72.6 54.2 %all-to-all-start = ((bf16[2,16,256,128]{3,1,0,2:T(8,128)(2,1)}), bf16[2,16,256,128]{3,1,0,2:T(8,128)(2,1)}, u32[]{:S(2)}, u32[]{:S(2)}) async-start(bf16[2,16,256,128]{3,1,0,2:T(8,128)(2,1)} %copy.82), calls=%async_computation | async-start | bytes 4194304 | tf_op jit(solution)/shard_map/all_to_all | solution.py:42
  79.3 3.8 copy-start.11
  81.7 1.4 copy-start.3
  126.8 54.3 %all-to-all-start.5 = ((bf16[2,256,16,128]{3,2,0,1:T(8,128)(2,1)}), bf16[2,256,16,128]{3,2,0,1:T(8,128)(2,1)}, u32[]{:S(2)}, u32[]{:S(2)}) async-start(bf16[2,256,16,128]{3,2,0,1:T(8,128)(2,1)} %copy.103), calls=%async_computation.5 | async-start | bytes 4194304 | tf_op jit(solution)/shard_map/all_to_all | solution.py:45
  136.0 1.4 copy-start.5
  181.1 54.4 %all-to-all-start.1 = ((bf16[2,256,16,128]{3,2,0,1:T(8,128)(2,1)}), bf16[2,256,16,128]{3,2,0,1:T(8,128)(2,1)}, u32[]{:S(2)}, u32[]{:S(2)}) async-start(bf16[2,256,16,128]{3,2,0,1:T(8,128)(2,1)} %copy.86), calls=%async_computation.1 | async-start | bytes 4194304 | tf_op jit(solution)/shard_map/all_to_all | solution.py:46
  237.4 2.2 copy-start.1
  237.4 2.9 copy-start.2
  245.3 54.3 %all-to-all-start.6 = ((bf16[2,16,256,128]{3,1,0,2:T(8,128)(2,1)}), bf16[2,16,256,128]{3,1,0,2:T(8,128)(2,1)}, u32[]{:S(2)}, u32[]{:S(2)}) async-start(bf16[2,16,256,128]{3,1,0,2:T(8,128)(2,1)} %copy.109), calls=%async_computation.6 | async-start | bytes 4194304 | tf_op jit(solution)/shard_map/all_to_all | solution.py:55
  299.6 54.3 %all-to-all-start.2 = ((bf16[2,16,256,128]{3,1,0,2:T(8,128)(2,1)}), bf16[2,16,256,128]{3,1,0,2:T(8,128)(2,1)}, u32[]{:S(2)}, u32[]{:S(2)}) async-start(bf16[2,16,256,128]{3,1,0,2:T(8,128)(2,1)} %copy.89), calls=%async_computation.2 | async-start | bytes 4194304 | tf_op jit(solution)/shard_map/all_to_all | solution.py:56
  308.8 1.3 copy-start.7
  353.9 54.3 %all-to-all-start.7 = ((bf16[2,256,16,128]{3,2,0,1:T(8,128)(2,1)}), bf16[2,256,16,128]{3,2,0,1:T(8,128)(2,1)}, u32[]{:S(2)}, u32[]{:S(2)}) async-start(bf16[2,256,16,128]{3,2,0,1:T(8,128)(2,1)} %copy.113), calls=%async_computation.7 | async-start | bytes 4194304 | tf_op jit(solution)/shard_map/all_to_all | solution.py:62
  363.2 1.3 copy-start.8
  408.3 54.3 %all-to-all-start.3 = ((bf16[2,256,16,128]{3,2,0,1:T(8,128)(2,1)}), bf16[2,256,16,128]{3,2,0,1:T(8,128)(2,1)}, u32[]{:S(2)}, u32[]{:S(2)}) async-start(bf16[2,256,16,128]{3,2,0,1:T(8,128)(2,1)} %copy.93), calls=%async_computation.3 | async-start | bytes 4194304 | tf_op jit(solution)/shard_map/all_to_all | solution.py:63
  415.1 308.9 %all-reduce.3.cloned.1.call-start = ((), (), s32[]{:S(2)}) async-start(), calls=%async_computation.8 | async-start | bytes 1048576 | tf_op jit(solution)/shard_map/psum | solution.py:72
  421.7 2.0 copy-start.6
  423.6 3.0 copy-start.4
  423.6 3.0 copy-start.9
  462.6 3.7 copy-start.12
  464.9 1.3 copy-start.10
Sparse Core Ops, SparseCore 0:
  467.8 256.1 all-reduce.2
where the time goes:
time: 734 us; the launch traced here: 733 us
  waiting for transfers between devices  552 us (75%)
  local copies, waits for them, and re-layouts  69.9 us (10%)
  starting transfers between devices  57 us (8%)
  matrix products  26.5 us (4%)
  between operations  14.2 us (2%)
  other arithmetic  13.5 us (2%)
    psum x1, waiting for transfers between devices, on_device(): lax.psum((first_terms, second_terms), ('dp', 'seq'))  249 us
    all_to_all x1, waiting for transfers between devices, on_device(): lax.all_to_all(weighted_home, 'seq', split_axis=2, concat_axis=1, tiled=T...  43.2 us
    all_to_all x1, waiting for transfers between devices, on_device(): lax.all_to_all(within_mix, 'seq', split_axis=2, concat_axis=1, tiled=True)  41.4 us
    all_to_all x1, waiting for transfers between devices, on_device(): lax.all_to_all(grad_spectrum, 'seq', split_axis=1, concat_axis=2, tiled=T...  40.3 us
    all_to_all x1, waiting for transfers between devices, on_device(): lax.all_to_all(grad_weighted_home, 'seq', split_axis=2, concat_axis=1, ti...  36.8 us
    all_to_all x1, waiting for transfers between devices, on_device(): lax.all_to_all(returned_spread, 'seq', split_axis=1, concat_axis=2, tiled...  36.8 us
    all_to_all x1, waiting for transfers between devices, on_device(): lax.all_to_all(spectrum, 'seq', split_axis=1, concat_axis=2, tiled=True)  36.7 us
    all_to_all x1, waiting for transfers between devices, on_device(): lax.all_to_all(grad_within, 'seq', split_axis=2, concat_axis=1, tiled=True)  36.7 us
  transfers between devices with their start and end apart: 9, of which 9 were waited for; matrix products, arithmetic and copies ran while one was open for 11% of the time, Pallas kernels for 0%

commit v1 on v0

--- a/solution.py
+++ b/solution.py
@@ -36,7 +36,12 @@
     grads_cube = cotangent.reshape(batch_count, local_blocks, block_size, channels)
     kernel_cube = kernel.reshape(local_blocks, block_size, channels)
     within_mix = within_blocks(factor_one, inputs_cube).astype(jnp.bfloat16)
-    within_spread = lax.all_to_all(within_mix, "seq", split_axis=2, concat_axis=1, tiled=True)
+    within_spread = jnp.concatenate(
+        jax.lax.all_to_all(
+            jnp.stack(jnp.split(within_mix, jax.lax.axis_size("seq"), 2), axis=0), "seq", 0, 0
+        ),
+        1,
+    )
     spectrum = across_blocks(factor_two, within_spread).astype(jnp.bfloat16)
     grad_within = within_blocks(factor_one, grads_cube).astype(jnp.bfloat16)
     grad_spread = lax.all_to_all(grad_within, "seq", split_axis=2, concat_axis=1, tiled=True)

time: 734 us -> 786 us (1.071)
  local copies, waits for them, and re-layouts: 69.9 us -> 122 us
    another operation x1 -> x19, local copies, waits for them, and re-layouts: 1.92 us -> 41.4 us  [the longest x18 39.5 us: on_device(): jnp.stack(jnp.split(within_mix, jax.lax.axis_size('seq'), 2), axis=0)]
    unnamed x29 -> x52, local copies, waits for them, and re-layouts: 11.3 us -> 28.6 us
  transfers between devices with their start and end apart: 9 -> 9, of which waited for: 9 -> 9; matrix products, arithmetic and copies ran while one was open for 11% -> 10% of each run, Pallas kernels for 0% -> 0%
where the time goes in v1:
time: 786 us; the launch traced here: 784 us
  waiting for transfers between devices  552 us (70%)
  local copies, waits for them, and re-layouts  122 us (16%)
  starting transfers between devices  56.8 us (7%)
  matrix products  25.2 us (3%)
  between operations  14.3 us (2%)
  other arithmetic  13.5 us (2%)
    psum x1, waiting for transfers between devices, on_device(): lax.psum((first_terms, second_terms), ('dp', 'seq'))  249 us
    all_to_all x1, waiting for transfers between devices, on_device(): lax.all_to_all(weighted_home, 'seq', split_axis=2, concat_axis=1, tiled=T...  43.2 us
    all_to_all x1, waiting for transfers between devices, on_device(): jax.lax.all_to_all(jnp.stack(jnp.split(within_mix, jax.lax.axis_size('seq...  41.3 us
    all_to_all x1, waiting for transfers between devices, on_device(): lax.all_to_all(grad_spectrum, 'seq', split_axis=1, concat_axis=2, tiled=T...  40.3 us
    another operation x18, local copies, waits for them, and re-layouts, on_device(): jnp.stack(jnp.split(within_mix, jax.lax.axis_size('seq'), 2), axis=0)  39.5 us
    all_to_all x1, waiting for transfers between devices, on_device(): lax.all_to_all(grad_within, 'seq', split_axis=2, concat_axis=1, tiled=True)  37.1 us
    all_to_all x1, waiting for transfers between devices, on_device(): lax.all_to_all(returned_spread, 'seq', split_axis=1, concat_axis=2, tiled...  36.8 us
    all_to_all x1, waiting for transfers between devices, on_device(): lax.all_to_all(grad_weighted_home, 'seq', split_axis=2, concat_axis=1, ti...  36.8 us
  transfers between devices with their start and end apart: 9, of which 9 were waited for; matrix products, arithmetic and copies ran while one was open for 10% of the time, Pallas kernels for 0%

profile of v1, /device:TPU:2, one launch (start us, length us, event | category | flops | bytes accessed | tf_op | source)
XLA Modules:
  0.0 783.6 jit_solution(11918454290747151906)
XLA Ops:
  9.7 7.6 slice_bitcast_fusion
  66.5 9.0 %all-to-all-start.4 = ((bf16[16,2,16,16,128]{4,3,2,1,0:T(8,128)(2,1)}), bf16[16,2,16,16,128]{4,3,2,1,0:T(8,128)(2,1)}, u32[]{:S(2)}, u32[]{:S(2)}) async-start(bf16[16,2,16,16,128]{4,3,2,1,0:T(8,128)(2,1)} %constant_dynamic-update-slice_fusion), calls=%async_computation.4 | async-start | bytes 4194304 | tf_op jit(solution)/shard_map/all_to_all | solution.py:40
  77.6 4.5 copy.79
  82.2 41.3 %all-to-all-done.4 = bf16[16,2,16,16,128]{4,3,2,1,0:T(8,128)(2,1)} async-done(((bf16[16,2,16,16,128]{4,3,2,1,0:T(8,128)(2,1)}), bf16[16,2,16,16,128]{4,3,2,1,0:T(8,128)(2,1)}, u32[]{:S(2)}, u32[]{:S(2)}) %all-to-all-start.4) | async-done | bytes 2097184 | tf_op jit(solution)/shard_map/all_to_all | solution.py:40
  123.5 6.7 all-to-all-start
  136.0 4.6 copy.114
  140.6 37.1 %all-to-all-done = bf16[2,16,256,128]{3,1,0,2:T(8,128)(2,1)} async-done(((bf16[2,16,256,128]{3,1,0,2:T(8,128)(2,1)}), bf16[2,16,256,128]{3,1,0,2:T(8,128)(2,1)}, u32[]{:S(2)}, u32[]{:S(2)}) %all-to-all-start) | async-done | bytes 2097184 | tf_op jit(solution)/shard_map/all_to_all | solution.py:47
  177.7 6.8 all-to-all-start.5
  190.8 4.5 copy.83
  195.3 36.7 %all-to-all-done.5 = bf16[2,256,16,128]{3,2,0,1:T(8,128)(2,1)} async-done(((bf16[2,256,16,128]{3,2,0,1:T(8,128)(2,1)}), bf16[2,256,16,128]{3,2,0,1:T(8,128)(2,1)}, u32[]{:S(2)}, u32[]{:S(2)}) %all-to-all-start.5) | async-done | bytes 2097184 | tf_op jit(solution)/shard_map/all_to_all | solution.py:50
  232.0 6.8 all-to-all-start.1
  246.0 40.3 %all-to-all-done.1 = bf16[2,256,16,128]{3,2,0,1:T(8,128)(2,1)} async-done(((bf16[2,256,16,128]{3,2,0,1:T(8,128)(2,1)}), bf16[2,256,16,128]{3,2,0,1:T(8,128)(2,1)}, u32[]{:S(2)}, u32[]{:S(2)}) %all-to-all-start.1) | async-done | bytes 2097184 | tf_op jit(solution)/shard_map/all_to_all | solution.py:51
  296.2 6.9 all-to-all-start.6
  303.0 4.3 copy.86
  307.3 43.2 %all-to-all-done.6 = bf16[2,16,256,128]{3,1,0,2:T(8,128)(2,1)} async-done(((bf16[2,16,256,128]{3,1,0,2:T(8,128)(2,1)}), bf16[2,16,256,128]{3,1,0,2:T(8,128)(2,1)}, u32[]{:S(2)}, u32[]{:S(2)}) %all-to-all-start.6) | async-done | bytes 2097184 | tf_op jit(solution)/shard_map/all_to_all | solution.py:60
  350.5 6.8 all-to-all-start.2
  363.5 4.6 copy.124
  368.1 36.8 %all-to-all-done.2 = bf16[2,16,256,128]{3,1,0,2:T(8,128)(2,1)} async-done(((bf16[2,16,256,128]{3,1,0,2:T(8,128)(2,1)}), bf16[2,16,256,128]{3,1,0,2:T(8,128)(2,1)}, u32[]{:S(2)}, u32[]{:S(2)}) %all-to-all-start.2) | async-done | bytes 2097184 | tf_op jit(solution)/shard_map/all_to_all | solution.py:61
  404.8 6.8 all-to-all-start.7
  417.9 4.5 copy.90
  422.4 36.8 %all-to-all-done.7 = bf16[2,256,16,128]{3,2,0,1:T(8,128)(2,1)} async-done(((bf16[2,256,16,128]{3,2,0,1:T(8,128)(2,1)}), bf16[2,256,16,128]{3,2,0,1:T(8,128)(2,1)}, u32[]{:S(2)}, u32[]{:S(2)}) %all-to-all-start.7) | async-done | bytes 2097184 | tf_op jit(solution)/shard_map/all_to_all | solution.py:67
  459.2 6.8 all-to-all-start.3
  482.2 31.3 %all-to-all-done.3 = bf16[2,256,16,128]{3,2,0,1:T(8,128)(2,1)} async-done(((bf16[2,256,16,128]{3,2,0,1:T(8,128)(2,1)}), bf16[2,256,16,128]{3,2,0,1:T(8,128)(2,1)}, u32[]{:S(2)}, u32[]{:S(2)}) %all-to-all-start.3) | async-done | bytes 2097184 | tf_op jit(solution)/shard_map/all_to_all | solution.py:68
  526.3 248.7 %all-reduce.3.cloned.1.call-done = (f32[256,256]{1,0:T(8,128)}, f32[256,256]{1,0:T(8,128)}) async-done(((f32[256,256]{1,0:T(8,128)}, f32[256,256]{1,0:T(8,128)}), (f32[256,256]{1,0:T(8,128)}, f32[256,256]{1,0:T(8,128)})) %all-reduce.3.cloned.1.call-update) | async-done | bytes 524304 | tf_op jit(solution)/shard_map/psum | solution.py:77
  (100 shorter events, 125.7 us)
Async XLA Ops:
  7.2 68.3 %copy-start = (bf16[2,4096,128]{2,1,0:T(8,128)(2,1)S(1)}, bf16[2,4096,128]{2,1,0:T(8,128)(2,1)}, u32[]{:S(2)}) copy-start(bf16[2,4096,128]{2,1,0:T(8,128)(2,1)} %param.6) | copy-start | bytes 6291460
  49.2 12.6 %copy-start.17 = (bf16[1,2,16,16,128]{4,3,2,1,0:T(8,128)(2,1)S(1)}, bf16[1,2,16,16,128]{4,3,2,1,0:T(8,128)(2,1)}, u32[]{:S(2)}) copy-start(bf16[1,2,16,16,128]{4,3,2,1,0:T(8,128)(2,1)} %copy.105) | copy-start | bytes 393220
  49.2 13.3 %copy-start.16 = (bf16[1,2,16,16,128]{4,3,2,1,0:T(8,128)(2,1)S(1)}, bf16[1,2,16,16,128]{4,3,2,1,0:T(8,128)(2,1)}, u32[]{:S(2)}) copy-start(bf16[1,2,16,16,128]{4,3,2,1,0:T(8,128)(2,1)} %copy.106) | copy-start | bytes 393220
  49.2 14.0 %copy-start.15 = (bf16[1,2,16,16,128]{4,3,2,1,0:T(8,128)(2,1)S(1)}, bf16[1,2,16,16,128]{4,3,2,1,0:T(8,128)(2,1)}, u32[]{:S(2)}) copy-start(bf16[1,2,16,16,128]{4,3,2,1,0:T(8,128)(2,1)} %copy.107) | copy-start | bytes 393220
  49.2 14.6 %copy-start.14 = (bf16[1,2,16,16,128]{4,3,2,1,0:T(8,128)(2,1)S(1)}, bf16[1,2,16,16,128]{4,3,2,1,0:T(8,128)(2,1)}, u32[]{:S(2)}) copy-start(bf16[1,2,16,16,128]{4,3,2,1,0:T(8,128)(2,1)} %copy.108) | copy-start | bytes 393220
  66.5 9.0 %copy-start.13 = (bf16[256,256]{1,0:T(8,128)(2,1)S(1)}, bf16[256,256]{1,0:T(8,128)(2,1)}, u32[]{:S(2)}) copy-start(bf16[256,256]{1,0:T(8,128)(2,1)} %param.8) | copy-start | bytes 393220
  66.5 57.0 %all-to-all-start.4 = ((bf16[16,2,16,16,128]{4,3,2,1,0:T(8,128)(2,1)}), bf16[16,2,16,16,128]{4,3,2,1,0:T(8,128)(2,1)}, u32[]{:S(2)}, u32[]{:S(2)}) async-start(bf16[16,2,16,16,128]{4,3,2,1,0:T(8,128)(2,1)} %constant_dynamic-update-slice_fusion), calls=%async_computation.4 | async-start | bytes 4194304 | tf_op jit(solution)/shard_map/all_to_all | solution.py:40
  123.5 54.2 %all-to-all-start = ((bf16[2,16,256,128]{3,1,0,2:T(8,128)(2,1)}), bf16[2,16,256,128]{3,1,0,2:T(8,128)(2,1)}, u32[]{:S(2)}, u32[]{:S(2)}) async-start(bf16[2,16,256,128]{3,1,0,2:T(8,128)(2,1)} %copy.79), calls=%async_computation | async-start | bytes 4194304 | tf_op jit(solution)/shard_map/all_to_all | solution.py:47
  130.2 3.4 copy-start.11
  132.2 1.4 copy-start.3
  177.7 54.3 %all-to-all-start.5 = ((bf16[2,256,16,128]{3,2,0,1:T(8,128)(2,1)}), bf16[2,256,16,128]{3,2,0,1:T(8,128)(2,1)}, u32[]{:S(2)}, u32[]{:S(2)}) async-start(bf16[2,256,16,128]{3,2,0,1:T(8,128)(2,1)} %copy.114), calls=%async_computation.5 | async-start | bytes 4194304 | tf_op jit(solution)/shard_map/all_to_all | solution.py:50
  186.9 1.4 copy-start.5
  232.0 54.3 %all-to-all-start.1 = ((bf16[2,256,16,128]{3,2,0,1:T(8,128)(2,1)}), bf16[2,256,16,128]{3,2,0,1:T(8,128)(2,1)}, u32[]{:S(2)}, u32[]{:S(2)}) async-start(bf16[2,256,16,128]{3,2,0,1:T(8,128)(2,1)} %copy.83), calls=%async_computation.1 | async-start | bytes 4194304 | tf_op jit(solution)/shard_map/all_to_all | solution.py:51
  288.2 2.2 copy-start.1
  288.3 2.9 copy-start.2
  296.2 54.3 %all-to-all-start.6 = ((bf16[2,16,256,128]{3,1,0,2:T(8,128)(2,1)}), bf16[2,16,256,128]{3,1,0,2:T(8,128)(2,1)}, u32[]{:S(2)}, u32[]{:S(2)}) async-start(bf16[2,16,256,128]{3,1,0,2:T(8,128)(2,1)} %copy.120), calls=%async_computation.6 | async-start | bytes 4194304 | tf_op jit(solution)/shard_map/all_to_all | solution.py:60
  350.5 54.3 %all-to-all-start.2 = ((bf16[2,16,256,128]{3,1,0,2:T(8,128)(2,1)}), bf16[2,16,256,128]{3,1,0,2:T(8,128)(2,1)}, u32[]{:S(2)}, u32[]{:S(2)}) async-start(bf16[2,16,256,128]{3,1,0,2:T(8,128)(2,1)} %copy.86), calls=%async_computation.2 | async-start | bytes 4194304 | tf_op jit(solution)/shard_map/all_to_all | solution.py:61
  404.8 54.3 %all-to-all-start.7 = ((bf16[2,256,16,128]{3,2,0,1:T(8,128)(2,1)}), bf16[2,256,16,128]{3,2,0,1:T(8,128)(2,1)}, u32[]{:S(2)}, u32[]{:S(2)}) async-start(bf16[2,256,16,128]{3,2,0,1:T(8,128)(2,1)} %copy.124), calls=%async_computation.7 | async-start | bytes 4194304 | tf_op jit(solution)/shard_map/all_to_all | solution.py:67
  459.2 54.3 %all-to-all-start.3 = ((bf16[2,256,16,128]{3,2,0,1:T(8,128)(2,1)}), bf16[2,256,16,128]{3,2,0,1:T(8,128)(2,1)}, u32[]{:S(2)}, u32[]{:S(2)}) async-start(bf16[2,256,16,128]{3,2,0,1:T(8,128)(2,1)} %copy.90), calls=%async_computation.3 | async-start | bytes 4194304 | tf_op jit(solution)/shard_map/all_to_all | solution.py:68
  466.0 308.9 %all-reduce.3.cloned.1.call-start = ((), (), s32[]{:S(2)}) async-start(), calls=%async_computation.8 | async-start | bytes 1048576 | tf_op jit(solution)/shard_map/psum | solution.py:77
  472.4 2.0 copy-start.6
  474.3 3.0 copy-start.4
  474.3 3.0 copy-start.9
  513.5 3.7 copy-start.12
  (3 other events, 4.0 us)
Sparse Core Ops, SparseCore 0:
  518.8 256.1 all-reduce.2
